TPU v7x, 256 devices: a whole 4x4x8 slice. The times are simulated.
256 devices in a mesh: blk: 8 (over y_lo, x), head: 32 (over z, y_hi, core).
Axes of the slice: x: 4, y: 4 (y_hi: 2, y_lo: 2; y = y_hi * 2 + y_lo), z: 8, core: 2. Of those that a mesh axis runs over, the one named last changes fastest.
Arguments:
- queries: bfloat16 [32768, 2048], P(('blk', 'head')), may hold values from -11 to 11
- keys: bfloat16 [32768, 2048], P(('blk', 'head')), may hold values from -11 to 11
- values: bfloat16 [32768, 2048], P(('blk', 'head')), may hold values from -6 to 6
- slopes: float32 [32], replicated, may hold values from 0.25 to 2
- layer: int32 [256], replicated, may hold values from 0 to 3, as said below
- mask: int32 [256, 256], replicated, may hold values from 0 to 1, as said below
- perm: int32 [256], replicated, may hold values from 0 to 255, as said below
Outputs:
- attended: bfloat16 [32768, 2048], P(('blk', 'head'))
Inputs may be any that keep to these rules, and one draw needn't show every extreme that they name: Block c means slots c * 32 to (c + 1) * 32 - 1; a tile is active if its layer is 3. Each tile may attend to itself. mask[perm[p], perm[q]] is 0 unless the block of q is the block of p or the one before or after it, the last and the first block counting as neighbours. In each of these three blocks a tile may attend to at least one tile, to at most 9 if it is active and to at most 3 otherwise; both bounds are reached. `layer`: every block holds at most 16 slots whose tile is active, and some block holds exactly 16. `perm`: A permutation of the tiles.
All inputs are finite; a program needn't handle non-finite values.
Results may differ from a plain program's by a relative error of at most 0.0065.
Values may be sent and summed in bfloat16 or wider, within the bound.
No kernel may reach another device: no remote copies, remote signals or barrier semaphores. Data moves between devices by JAX's collectives and lax.ppermute only.
A program may use at most 64 MiB of HBM per device.

v0:
```python
import math

import jax
import jax.numpy as jnp
from jax import lax
from jax.experimental import pallas as pl
from jax.experimental.pallas import tpu as pltpu
from jax.sharding import PartitionSpec as P

HD = 64
HEADS = 32
TILE = 128
TB = 32
TILES = 256
KCAP = 9
GROUP = 3
UNROLL = 3
MOST_STEPS = 256
LOWEST = -1e30
EXPONENT = math.log2(math.e)

f32 = jnp.float32
bf16 = jnp.bfloat16
i32 = jnp.int32


def from_behind(value, axis, steps):
    count = lax.axis_size(axis)
    pairs = [(source, (source + steps) % count) for source in range(count)]
    return lax.ppermute(value, axis, pairs)


def pack_kv_kernel(k_ref, v_ref, kv_ref):
    for pair in range(HEADS // 2):
        columns = slice(pair * 128, pair * 128 + 128)
        k = k_ref[:, columns]
        upper, lower = k[:64], k[64:]
        kv_ref[2 * pair, :64, :] = jnp.concatenate([upper[:, :64], lower[:, :64]], axis=1)
        kv_ref[2 * pair + 1, :64, :] = jnp.concatenate([upper[:, 64:], lower[:, 64:]], axis=1)
        v = v_ref[:, columns].T
        kv_ref[2 * pair, 64:, :] = v[:64]
        kv_ref[2 * pair + 1, 64:, :] = v[64:]


def pack_kv(keys, values):
    return pl.pallas_call(
        pack_kv_kernel,
        out_shape=jax.ShapeDtypeStruct((HEADS, 128, 128), bf16),
        name="pack_kv",
    )(keys, values)


def pack_q_kernel(q_ref, out_ref):
    for pair in range(HEADS // 2):
        q = q_ref[:, pair * 128 : pair * 128 + 128].T
        out_ref[2 * pair] = q[:64]
        out_ref[2 * pair + 1] = q[64:]


def pack_q(queries):
    return pl.pallas_call(
        pack_q_kernel,
        out_shape=jax.ShapeDtypeStruct((HEADS, HD, 128), bf16),
        name="pack_q",
    )(queries)


def unpack_kernel(in_ref, out_ref):
    for pair in range(HEADS // 2):
        both = jnp.concatenate([in_ref[2 * pair], in_ref[2 * pair + 1]], axis=0)
        out_ref[:, pair * 128 : pair * 128 + 128] = both.T


def unpack(array):
    return pl.pallas_call(
        unpack_kernel,
        out_shape=jax.ShapeDtypeStruct((128, HEADS * HD), bf16),
        name="unpack",
    )(array)


def iota(shape, dim):
    return lax.broadcasted_iota(i32, shape, dim)


def exact_dot(a, b):
    return jnp.dot(a.astype(bf16), b.astype(bf16), preferred_element_type=f32)


def table_kernel(block_ref, perm_ref, layer_ref, mask_ref, out_ref):
    block = block_ref[0]
    shift = lax.rem(TILES + TB - block * TB, TILES)
    perm = pltpu.roll(jnp.broadcast_to(perm_ref[...], (8, TILES)), shift, 1)[:1, :128]
    select = (perm == iota((TILES, 128), 0)).astype(f32)
    select_t = select.T
    own_select = select_t[TB : 2 * TB]
    columns = exact_dot(mask_ref[...].astype(f32), select)
    allowed = exact_dot(own_select, columns)
    allowed = jnp.where(iota((TB, 128), 1) < 3 * TB, allowed, 0.0)
    layer = layer_ref[...].astype(f32)
    layer_row = exact_dot(jnp.broadcast_to(layer, (8, TILES)), select)[:1]
    layer_own = jnp.sum(own_select * layer, axis=1, keepdims=True)
    gap = jnp.abs(layer_own - layer_row)
    before = (iota((128, 128), 0) < iota((128, 128), 1)).astype(f32)
    place = exact_dot(allowed, before)
    place = jnp.where(allowed > 0.5, place, 200.0)
    count = jnp.sum(allowed, axis=1, keepdims=True)
    steps = jnp.zeros((TB, 1), f32)
    for filled in range(0, 3 * KCAP, GROUP):
        steps = steps + (count > filled + 0.5).astype(f32)
    steps = jnp.broadcast_to(steps, (TB, 128))
    earlier = (iota((TB, TB), 1) < iota((TB, TB), 0)).astype(f32)
    start = exact_dot(earlier, steps)
    start = jnp.concatenate([start, start], axis=1)
    steps = jnp.concatenate([steps, steps], axis=1)
    now = iota((TB, MOST_STEPS), 1).astype(f32)
    hit = ((start <= now) & (now < start + steps)).astype(f32)
    covered = jnp.sum(hit, axis=0, keepdims=True)
    own_tile = jnp.sum(hit * iota((TB, MOST_STEPS), 0).astype(f32), axis=0, keepdims=True)
    own_tile = jnp.where(covered > 0.5, own_tile, TB - 1.0)
    within = jnp.sum(hit * (now - start), axis=0, keepdims=True)
    opening = (covered > 0.5) & (within < 0.5)
    total = jnp.sum(steps, axis=0, keepdims=True)
    place_t = exact_dot(place.T, hit)
    gap_t = exact_dot(gap.T, hit)
    tile = iota((128, MOST_STEPS), 0).astype(f32)
    rows = [own_tile, opening.astype(f32), total]
    gaps = []
    for g in range(GROUP):
        chosen = ((place_t == within * GROUP + g) & (covered > 0.5)).astype(f32)
        present = jnp.sum(chosen, axis=0, keepdims=True)
        rows.append(jnp.sum(chosen * tile, axis=0, keepdims=True))
        gaps.append(jnp.where(present > 0.5, jnp.sum(chosen * gap_t, axis=0, keepdims=True), -1.0))
    rows = rows + gaps
    rows = rows + [jnp.zeros((1, MOST_STEPS), f32)] * (16 - len(rows))
    out_ref[...] = jnp.concatenate(rows, axis=0).astype(i32)


def table(block, perm, layer, mask):
    return pl.pallas_call(
        table_kernel,
        out_shape=jax.ShapeDtypeStruct((16, MOST_STEPS), i32),
        in_specs=[pl.BlockSpec(memory_space=pltpu.SMEM)] + [pl.BlockSpec(memory_space=pltpu.VMEM)] * 3,
        out_specs=pl.BlockSpec(memory_space=pltpu.VMEM),
        name="table",
    )(block, perm.reshape(1, TILES), layer.reshape(1, TILES), mask)


def attend_kernel(
    table_ref,
    slope_ref,
    q_ref,
    prior_ref,
    own_ref,
    later_ref,
    out_ref,
    kv,
    arrived,
    *buffers,
):
    scores, weights = buffers[: 2 * UNROLL], buffers[2 * UNROLL :]
    copies = [
        pltpu.make_async_copy(source, kv.at[pl.ds(index * TB, TB)], arrived.at[index])
        for index, source in enumerate((prior_ref, own_ref, later_ref))
    ]
    for copy in copies:
        copy.start()
    scale = EXPONENT / math.sqrt(HD)
    slope = slope_ref[0] * EXPONENT
    total_steps = table_ref[2, 0]
    zeros = jnp.zeros((HD, TILE), bf16)
    for copy in copies:
        copy.wait()

    def score(step, into):
        q = q_ref[table_ref[0, step]]
        q = jnp.concatenate(
            [jnp.concatenate([q, zeros], axis=1), jnp.concatenate([zeros, q], axis=1)], axis=0
        )
        k = jnp.concatenate([kv[table_ref[3 + g, step], :HD, :] for g in range(GROUP)], axis=0)
        into[...] = jnp.dot(k, q, preferred_element_type=f32)

    def weigh(step, source, into, top):
        first = table_ref[1, step] == 1
        biases = []
        top = jnp.where(first, LOWEST, top)
        new_top = top
        for g in range(GROUP):
            gap = table_ref[3 + GROUP + g, step]
            biases.append(jnp.where(gap < 0, -LOWEST, slope * gap.astype(f32)))
            s = source[g * HD : g * HD + HD, :]
            s = jnp.maximum(s[:, :TILE], s[:, TILE:])
            s = jnp.max(s, axis=0, keepdims=True) * scale - biases[g]
            new_top = jnp.maximum(new_top, s)
        for g in range(GROUP):
            s = source[g * HD : g * HD + HD, :]
            offset = new_top + biases[g]
            for half in range(2):
                w = jnp.exp2(s[:, half * TILE : half * TILE + TILE] * scale - offset)
                row = g * TILE + half * HD
                into[row : row + HD, :] = w.astype(bf16)
        return new_top, jnp.where(first, 0.0, jnp.exp2(top - new_top))

    def gather(step, source, fade, mixed):
        v = jnp.concatenate([kv[table_ref[3 + g, step], HD:, :] for g in range(GROUP)], axis=1)
        v = jnp.concatenate([v, ones], axis=0)
        mixed = mixed * fade + jnp.dot(v, source[...], preferred_element_type=f32)
        out_ref[table_ref[0, step]] = (mixed[:HD] * (1.0 / mixed[HD : HD + 1])).astype(bf16)
        return mixed

    def body(pair, carry):
        top, mixed, fades = carry
        for parity in range(2):
            trip = pair * 2 + parity
            for u in range(UNROLL):
                step = jnp.maximum((trip - 2) * UNROLL + u, 0)
                mixed = gather(step, weights[parity * UNROLL + u], fades[parity * UNROLL + u], mixed)
            for u in range(UNROLL):
                step = jnp.maximum((trip - 1) * UNROLL + u, 0)
                slot = (1 - parity) * UNROLL + u
                top, fade = weigh(step, scores[slot], weights[slot], top)
                fades = fades[:slot] + (fade,) + fades[slot + 1 :]
            for u in range(UNROLL):
                score(trip * UNROLL + u, scores[parity * UNROLL + u])
        return top, mixed, fades

    row = jnp.zeros((1, TILE), f32)
    ones = jnp.ones((16, GROUP * TILE), bf16)
    for slot in range(UNROLL, 2 * UNROLL):
        scores[slot][...] = jnp.zeros_like(scores[slot])
    for ref in weights:
        ref[...] = jnp.zeros_like(ref)
    pairs = lax.div(total_steps + 4 * UNROLL - 1, 2 * UNROLL)
    lax.fori_loop(0, pairs, body, (row, jnp.zeros((HD + 16, TILE), f32), (row,) * (2 * UNROLL)))


def attend(steps, slope, q, prior, own, later):
    smem = pl.BlockSpec(memory_space=pltpu.SMEM)
    vmem = pl.BlockSpec(memory_space=pltpu.VMEM)
    anywhere = pl.BlockSpec(memory_space=pl.ANY)
    return pl.pallas_call(
        attend_kernel,
        out_shape=jax.ShapeDtypeStruct((TB, HD, TILE), bf16),
        in_specs=[smem, smem, vmem, anywhere, anywhere, anywhere],
        out_specs=vmem,
        scratch_shapes=[
            pltpu.VMEM((3 * TB, 2 * HD, TILE), bf16),
            pltpu.SemaphoreType.DMA((3,)),
        ]
        + [pltpu.VMEM((GROUP * HD, 2 * TILE), f32)] * (2 * UNROLL)
        + [pltpu.VMEM((GROUP * TILE, TILE), bf16)] * (2 * UNROLL),
        name="attend",
    )(steps, slope, q, prior, own, later)


def exchange(array):
    return lax.all_to_all(array, "head", split_axis=0, concat_axis=0, tiled=True)


def per_device(queries, keys, values, slopes, layer, mask, perm):
    block = lax.axis_index("blk").astype(i32).reshape(1)
    slope = lax.dynamic_slice_in_dim(slopes, lax.axis_index("head"), 1)
    own = exchange(pack_kv(keys, values))
    packed = pack_q(queries)
    steps = table(block, perm, layer, mask)
    own, packed, steps = lax.optimization_barrier((own, packed, steps))
    prior = from_behind(own, "blk", 1)
    later = from_behind(own, "blk", -1)
    q = exchange(packed)
    mixed = attend(steps, slope, q, prior, own, later)
    return unpack(exchange(mixed))


def solution(mesh):
    rows = P(("blk", "head"), None)
    return jax.shard_map(
        per_device,
        mesh=mesh,
        in_specs=(rows, rows, rows, P(), P(), P(), P()),
        out_specs=rows,
        check_vma=False,
    )
```

profile of v0, /device:TPU:1, one launch (start us, length us, event | category | flops | bytes accessed | tf_op | source)
XLA Modules:
  0.0 117.7 jit_solution(3639288923360751037)
XLA Ops:
  0.0 2.5 %pack_kv.1 = bf16[32,128,128]{2,1,0:T(8,128)(2,1)} custom-call(bf16[128,2048]{1,0:T(8,128)(2,1)} %k_ref.1, bf16[128,2048]{1,0:T(8,128)(2,1)} %v_ref.1), custom_call_target="tpu_custom_call" | custom-call | tf_op jit(solution)/shard_map/pack_kv/pallas_call | solution.py:46
  2.5 12.8 %all-to-all-start = ((bf16[32,128,128]{2,1,0:T(8,128)(2,1)}), bf16[32,128,128]{2,1,0:T(8,128)(2,1)S(1)}, u32[]{:S(2)}, u32[]{:S(2)}) async-start(bf16[32,128,128]{2,1,0:T(8,128)(2,1)} %pack_kv.1), calls=%async_computation | async-start | bytes 2097152 | tf_op jit(solution)/shard_map/all_to_all | solution.py:257
  15.3 2.0 %pack_q.1 = bf16[32,64,128]{2,1,0:T(8,128)(2,1)} custom-call(bf16[128,2048]{1,0:T(8,128)(2,1)} %q_ref.1), custom_call_target="tpu_custom_call" | custom-call | tf_op jit(solution)/shard_map/pack_q/pallas_call | solution.py:61
  17.3 2.4 %table.1.table_ref = s32[16,256]{1,0:T(8,128)} custom-call(s32[1]{0:T(128)} %bitcast.block_ref, s32[1,256]{1,0:T(1,128)} %bitcast.3, s32[1,256]{1,0:T(1,128)} %bitcast.4, s32[256,256]{1,0:T(8,128)} %mask_ref.1), custom_call_target="tpu_custom_call" | custom-call | tf_op jit(solution)/shard_map/table/pallas_call | solution.py:140
  19.8 23.7 %all-to-all-done.own_ref = bf16[32,128,128]{2,1,0:T(8,128)(2,1)S(1)} async-done(((bf16[32,128,128]{2,1,0:T(8,128)(2,1)}), bf16[32,128,128]{2,1,0:T(8,128)(2,1)S(1)}, u32[]{:S(2)}, u32[]{:S(2)}) %all-to-all-start) | async-done | bytes 1048608 | tf_op jit(solution)/shard_map/all_to_all | solution.py:257
  43.4 0.0 copy-start
  43.4 2.6 %collective-permute-start.1 = (bf16[32,128,128]{2,1,0:T(8,128)(2,1)S(1)}, bf16[32,128,128]{2,1,0:T(8,128)(2,1)S(1)}, u32[]{:S(2)}, u32[]{:S(2)}) collective-permute-start(bf16[32,128,128]{2,1,0:T(8,128)(2,1)S(1)} %all-to-all-done.own_ref), channel_id=1, source_target_pairs={{0,224},{32,0},{64,32},{96,64},{128,96},{160,128},{192,160},{224,1... | collective-permute-start | bytes 3145736 | tf_op jit(solution)/shard_map/ppermute | solution.py:30
  46.0 0.0 collective-permute-start
  46.0 6.7 %all-to-all-start.1 = ((bf16[32,64,128]{2,1,0:T(8,128)(2,1)}), bf16[32,64,128]{2,1,0:T(8,128)(2,1)S(1)}, u32[]{:S(2)}, u32[]{:S(2)}) async-start(bf16[32,64,128]{2,1,0:T(8,128)(2,1)} %pack_q.1), calls=%async_computation.1 | async-start | bytes 1048576 | tf_op jit(solution)/shard_map/all_to_all | solution.py:257
  52.7 0.0 copy-start.3
  52.7 0.6 copy-done.3
  53.4 0.6 dynamic_slice.3.slope_ref
  53.9 27.3 %all-to-all-done.1.q_ref = bf16[32,64,128]{2,1,0:T(8,128)(2,1)S(1)} async-done(((bf16[32,64,128]{2,1,0:T(8,128)(2,1)}), bf16[32,64,128]{2,1,0:T(8,128)(2,1)S(1)}, u32[]{:S(2)}, u32[]{:S(2)}) %all-to-all-start.1) | async-done | bytes 524320 | tf_op jit(solution)/shard_map/all_to_all | solution.py:257
  81.2 0.0 copy-start.1
  81.2 0.0 collective-permute-done.1.later_ref
  81.2 0.0 copy-start.2
  81.2 0.0 collective-permute-done.prior_ref
  81.2 0.0 copy-done
  81.3 0.8 copy-done.1
  82.0 0.4 copy-done.2
  82.4 11.0 %attend.1 = bf16[32,64,128]{2,1,0:T(8,128)(2,1)} custom-call(s32[16,256]{1,0:T(8,128)} %table.1.table_ref, f32[1]{0:T(128)} %dynamic_slice.3.slope_ref, bf16[32,64,128]{2,1,0:T(8,128)(2,1)} %copy-done.1, bf16[32,128,128]{2,1,0:T(8,128)(2,1)} %collective-permute-done.prior_ref, bf16[32,128,128]{2,1,0:T(8,128)(2,1)} %copy-done, bf16[32,128,128]{2,1,0:T(8,128)(2,1)} %copy-done.2), custom_call_target="tpu_custom_call" | custom-call | tf_op jit(solution)/shard_map/attend/pallas_call | solution.py:241
  93.4 22.3 %all_to_all.15.in_ref = bf16[32,64,128]{2,1,0:T(8,128)(2,1)} all-to-all(bf16[32,64,128]{2,1,0:T(8,128)(2,1)} %attend.1), channel_id=1, replica_groups=mesh['blk'=8,'head'=32] {'head'}, dimensions={0} | all-to-all | bytes 1048576 | tf_op jit(solution)/shard_map/all_to_all | solution.py:257
  115.7 2.0 %unpack.1 = bf16[128,2048]{1,0:T(8,128)(2,1)} custom-call(bf16[32,64,128]{2,1,0:T(8,128)(2,1)} %all_to_all.15.in_ref), custom_call_target="tpu_custom_call" | custom-call | tf_op jit(solution)/shard_map/unpack/pallas_call | solution.py:75
Async XLA Ops:
  2.5 40.9 %all-to-all-start = ((bf16[32,128,128]{2,1,0:T(8,128)(2,1)}), bf16[32,128,128]{2,1,0:T(8,128)(2,1)S(1)}, u32[]{:S(2)}, u32[]{:S(2)}) async-start(bf16[32,128,128]{2,1,0:T(8,128)(2,1)} %pack_kv.1), calls=%async_computation | async-start | bytes 2097152 | tf_op jit(solution)/shard_map/all_to_all | solution.py:257
  43.4 37.8 %copy-start = (bf16[32,128,128]{2,1,0:T(8,128)(2,1)}, bf16[32,128,128]{2,1,0:T(8,128)(2,1)S(1)}, u32[]{:S(2)}) copy-start(bf16[32,128,128]{2,1,0:T(8,128)(2,1)S(1)} %all-to-all-done.own_ref) | copy-start | bytes 3145732
  43.4 37.8 %collective-permute-start.1 = (bf16[32,128,128]{2,1,0:T(8,128)(2,1)S(1)}, bf16[32,128,128]{2,1,0:T(8,128)(2,1)S(1)}, u32[]{:S(2)}, u32[]{:S(2)}) collective-permute-start(bf16[32,128,128]{2,1,0:T(8,128)(2,1)S(1)} %all-to-all-done.own_ref), channel_id=1, source_target_pairs={{0,224},{32,0},{64,32},{96,64},{128,96},{160,128},{192,160},{224,1... | collective-permute-start | bytes 3145736 | tf_op jit(solution)/shard_map/ppermute | solution.py:30
  46.0 35.2 %collective-permute-start = (bf16[32,128,128]{2,1,0:T(8,128)(2,1)S(1)}, bf16[32,128,128]{2,1,0:T(8,128)(2,1)}, u32[]{:S(2)}, u32[]{:S(2)}) collective-permute-start(bf16[32,128,128]{2,1,0:T(8,128)(2,1)S(1)} %all-to-all-done.own_ref), channel_id=1, source_target_pairs={{0,32},{32,64},{64,96},{96,128},{128,160},{160,192},{192,224},{224... | collective-permute-start | bytes 3145736 | tf_op jit(solution)/shard_map/ppermute | solution.py:30
  46.0 35.2 %all-to-all-start.1 = ((bf16[32,64,128]{2,1,0:T(8,128)(2,1)}), bf16[32,64,128]{2,1,0:T(8,128)(2,1)S(1)}, u32[]{:S(2)}, u32[]{:S(2)}) async-start(bf16[32,64,128]{2,1,0:T(8,128)(2,1)} %pack_q.1), calls=%async_computation.1 | async-start | bytes 1048576 | tf_op jit(solution)/shard_map/all_to_all | solution.py:257
  52.7 0.7 copy-start.3
  81.2 0.8 copy-start.1
  81.2 1.1 copy-start.2
where the time goes:
time: 119 us; the launch traced here: 118 us
  waiting for transfers between devices  51 us (43%)
  blocking collectives  22.3 us (19%)
  starting transfers between devices  22 us (18%)
  Pallas kernels  20.1 us (17%)
  local copies, waits for them, and re-layouts  2.37 us (2%)
    all_to_all x2, waiting for transfers between devices, exchange(): lax.all_to_all(array, 'head', split_axis=0, concat_axis=0, tiled=True)  50.9 us
    all_to_all x1, blocking collectives, exchange(): lax.all_to_all(array, 'head', split_axis=0, concat_axis=0, tiled=True)  22.3 us
    all_to_all x2, starting transfers between devices, exchange(): lax.all_to_all(array, 'head', split_axis=0, concat_axis=0, tiled=True)  19.4 us
    pallas_call x1, Pallas kernels, attend(): pl.pallas_call(attend_kernel, out_shape=jax.ShapeDtypeStruct((TB, HD, TIL...  11 us
    ppermute x2, starting transfers between devices, from_behind(): return lax.ppermute(value, axis, pairs)  2.59 us
    pallas_call x1, Pallas kernels, pack_kv(): pl.pallas_call(pack_kv_kernel, out_shape=jax.ShapeDtypeStruct((HEADS, 128...  2.51 us
    pallas_call x1, Pallas kernels, table(): pl.pallas_call(table_kernel, out_shape=jax.ShapeDtypeStruct((16, MOST_STE...  2.45 us
  transfers between devices with their start and end apart: 4, of which 2 were waited for; matrix products, arithmetic and copies ran while one was open for 0% of the time, Pallas kernels for 4%

commit v1 on v0

--- a/solution.py
+++ b/solution.py
@@ -15,6 +15,7 @@
 KCAP = 9
 GROUP = 3
 UNROLL = 3
+PARTS = 2
 MOST_STEPS = 256
 LOWEST = -1e30
 EXPONENT = math.log2(math.e)
@@ -30,22 +31,48 @@
     return lax.ppermute(value, axis, pairs)
 
 
-def pack_kv_kernel(k_ref, v_ref, kv_ref):
-    for pair in range(HEADS // 2):
-        columns = slice(pair * 128, pair * 128 + 128)
-        k = k_ref[:, columns]
-        upper, lower = k[:64], k[64:]
-        kv_ref[2 * pair, :64, :] = jnp.concatenate([upper[:, :64], lower[:, :64]], axis=1)
-        kv_ref[2 * pair + 1, :64, :] = jnp.concatenate([upper[:, 64:], lower[:, 64:]], axis=1)
-        v = v_ref[:, columns].T
-        kv_ref[2 * pair, 64:, :] = v[:64]
-        kv_ref[2 * pair + 1, 64:, :] = v[64:]
+def pack_kv_kernel(k_hbm, v_hbm, kv_hbm, k_ref, v_ref, kv_ref, k_sem, v_sem, kv_sem):
+    width = HEADS * HD // PARTS
+    heads = HEADS // PARTS
+    loads, stores = [], []
+    for part in range(PARTS):
+        columns = pl.ds(part * width, width)
+        k_load = pltpu.make_async_copy(k_hbm.at[:, columns], k_ref.at[part], k_sem.at[part])
+        v_load = pltpu.make_async_copy(v_hbm.at[:, columns], v_ref.at[part], v_sem.at[part])
+        k_load.start()
+        v_load.start()
+        loads.append((k_load, v_load))
+    for part in range(PARTS):
+        loads[part][0].wait()
+        loads[part][1].wait()
+        for pair in range(heads // 2):
+            columns = slice(pair * 128, pair * 128 + 128)
+            one, two = part * heads + 2 * pair, part * heads + 2 * pair + 1
+            k = k_ref[part, :, columns]
+            upper, lower = k[:64], k[64:]
+            kv_ref[one, :64, :] = jnp.concatenate([upper[:, :64], lower[:, :64]], axis=1)
+            kv_ref[two, :64, :] = jnp.concatenate([upper[:, 64:], lower[:, 64:]], axis=1)
+            v = v_ref[part, :, columns].T
+            kv_ref[one, 64:, :] = v[:64]
+            kv_ref[two, 64:, :] = v[64:]
+        chunk = pl.ds(part * heads, heads)
+        store = pltpu.make_async_copy(kv_ref.at[chunk], kv_hbm.at[chunk], kv_sem.at[part])
+        store.start()
+        stores.append(store)
+    for store in stores:
+        store.wait()
 
 
 def pack_kv(keys, values):
+    anywhere = pl.BlockSpec(memory_space=pl.ANY)
     return pl.pallas_call(
         pack_kv_kernel,
         out_shape=jax.ShapeDtypeStruct((HEADS, 128, 128), bf16),
+        in_specs=[anywhere] * 2,
+        out_specs=anywhere,
+        scratch_shapes=[pltpu.VMEM((PARTS, 128, HEADS * HD // PARTS), bf16)] * 2
+        + [pltpu.VMEM((HEADS, 128, 128), bf16)]
+        + [pltpu.SemaphoreType.DMA((PARTS,))] * 3,
         name="pack_kv",
     )(keys, values)
 
@@ -75,6 +102,7 @@
     return pl.pallas_call(
         unpack_kernel,
         out_shape=jax.ShapeDtypeStruct((128, HEADS * HD), bf16),
+        compiler_params=pltpu.CompilerParams(vmem_limit_bytes=8 * 2**20),
         name="unpack",
     )(array)
 
@@ -249,6 +277,7 @@
         ]
         + [pltpu.VMEM((GROUP * HD, 2 * TILE), f32)] * (2 * UNROLL)
         + [pltpu.VMEM((GROUP * TILE, TILE), bf16)] * (2 * UNROLL),
+        compiler_params=pltpu.CompilerParams(vmem_limit_bytes=12 * 2**20),
         name="attend",
     )(steps, slope, q, prior, own, later)
 

time: 119 us -> 114 us (0.958)
  Pallas kernels: 20.1 us -> 17.1 us
    pallas_call x1, Pallas kernels: 11 us -> 9.38 us  [attend(): pl.pallas_call(attend_kernel, out_shape=jax.ShapeDtypeStruct((TB, HD, TIL...]
  transfers between devices with their start and end apart: 4 -> 4, of which waited for: 2 -> 2; matrix products, arithmetic and copies ran while one was open for 0% -> 1% of each run, Pallas kernels for 4% -> 4%
where the time goes in v1:
time: 114 us; the launch traced here: 113 us
  waiting for transfers between devices  50.8 us (45%)
  starting transfers between devices  22.2 us (19%)
  blocking collectives  21.9 us (19%)
  Pallas kernels  17.1 us (15%)
  local copies, waits for them, and re-layouts  1.25 us (1%)
    all_to_all x2, waiting for transfers between devices, exchange(): lax.all_to_all(array, 'head', split_axis=0, concat_axis=0, tiled=True)  50.8 us
    all_to_all x1, blocking collectives, exchange(): lax.all_to_all(array, 'head', split_axis=0, concat_axis=0, tiled=True)  21.9 us
    all_to_all x2, starting transfers between devices, exchange(): lax.all_to_all(array, 'head', split_axis=0, concat_axis=0, tiled=True)  19.6 us
    pallas_call x1, Pallas kernels, attend(): pl.pallas_call(attend_kernel, out_shape=jax.ShapeDtypeStruct((TB, HD, TIL...  9.38 us
    ppermute x2, starting transfers between devices, from_behind(): return lax.ppermute(value, axis, pairs)  2.59 us
    pallas_call x1, Pallas kernels, table(): pl.pallas_call(table_kernel, out_shape=jax.ShapeDtypeStruct((16, MOST_STE...  2.44 us
    pallas_call x1, Pallas kernels, pack_kv(): pl.pallas_call(pack_kv_kernel, out_shape=jax.ShapeDtypeStruct((HEADS, 128...  2.3 us
  transfers between devices with their start and end apart: 4, of which 2 were waited for; matrix products, arithmetic and copies ran while one was open for 1% of the time, Pallas kernels for 4%

profile of v1, /device:TPU:1, one launch (start us, length us, event | category | flops | bytes accessed | tf_op | source)
XLA Modules:
  0.0 113.4 jit_solution(16255625109768947515)
XLA Ops:
  0.0 2.3 %pack_kv.1 = bf16[32,128,128]{2,1,0:T(8,128)(2,1)} custom-call(bf16[128,2048]{1,0:T(8,128)(2,1)} %k_hbm.1, bf16[128,2048]{1,0:T(8,128)(2,1)} %v_hbm.1), custom_call_target="tpu_custom_call" | custom-call | tf_op jit(solution)/shard_map/pack_kv/pallas_call | solution.py:68
  2.3 12.8 %all-to-all-start = ((bf16[32,128,128]{2,1,0:T(8,128)(2,1)}), bf16[32,128,128]{2,1,0:T(8,128)(2,1)S(1)}, u32[]{:S(2)}, u32[]{:S(2)}) async-start(bf16[32,128,128]{2,1,0:T(8,128)(2,1)} %pack_kv.1), calls=%async_computation | async-start | bytes 2097152 | tf_op jit(solution)/shard_map/all_to_all | solution.py:286
  15.1 2.0 %pack_q.1 = bf16[32,64,128]{2,1,0:T(8,128)(2,1)} custom-call(bf16[128,2048]{1,0:T(8,128)(2,1)} %q_ref.1), custom_call_target="tpu_custom_call" | custom-call | tf_op jit(solution)/shard_map/pack_q/pallas_call | solution.py:88
  17.1 2.4 %table.1.table_ref = s32[16,256]{1,0:T(8,128)} custom-call(s32[1]{0:T(128)} %bitcast.block_ref, s32[1,256]{1,0:T(1,128)} %bitcast.3, s32[1,256]{1,0:T(1,128)} %bitcast.4, s32[256,256]{1,0:T(8,128)} %mask_ref.1), custom_call_target="tpu_custom_call" | custom-call | tf_op jit(solution)/shard_map/table/pallas_call | solution.py:168
  19.6 23.7 %all-to-all-done.own_ref = bf16[32,128,128]{2,1,0:T(8,128)(2,1)S(1)} async-done(((bf16[32,128,128]{2,1,0:T(8,128)(2,1)}), bf16[32,128,128]{2,1,0:T(8,128)(2,1)S(1)}, u32[]{:S(2)}, u32[]{:S(2)}) %all-to-all-start) | async-done | bytes 1048608 | tf_op jit(solution)/shard_map/all_to_all | solution.py:286
  43.2 2.6 %collective-permute-start.1 = (bf16[32,128,128]{2,1,0:T(8,128)(2,1)S(1)}, bf16[32,128,128]{2,1,0:T(8,128)(2,1)S(1)}, u32[]{:S(2)}, u32[]{:S(2)}) collective-permute-start(bf16[32,128,128]{2,1,0:T(8,128)(2,1)S(1)} %all-to-all-done.own_ref), channel_id=1, source_target_pairs={{0,224},{32,0},{64,32},{96,64},{128,96},{160,128},{192,160},{224,1... | collective-permute-start | bytes 3145736 | tf_op jit(solution)/shard_map/ppermute | solution.py:31
  45.8 0.0 collective-permute-start
  45.8 0.0 copy-start
  45.8 6.8 %all-to-all-start.1 = ((bf16[32,64,128]{2,1,0:T(8,128)(2,1)}), bf16[32,64,128]{2,1,0:T(8,128)(2,1)S(1)}, u32[]{:S(2)}, u32[]{:S(2)}) async-start(bf16[32,64,128]{2,1,0:T(8,128)(2,1)} %pack_q.1), calls=%async_computation.1 | async-start | bytes 1048576 | tf_op jit(solution)/shard_map/all_to_all | solution.py:286
  52.6 0.0 copy-start.1
  52.6 0.6 copy-done.1
  53.3 0.6 dynamic_slice.3.slope_ref
  53.9 27.1 %all-to-all-done.1.q_ref = bf16[32,64,128]{2,1,0:T(8,128)(2,1)S(1)} async-done(((bf16[32,64,128]{2,1,0:T(8,128)(2,1)}), bf16[32,64,128]{2,1,0:T(8,128)(2,1)S(1)}, u32[]{:S(2)}, u32[]{:S(2)}) %all-to-all-start.1) | async-done | bytes 524320 | tf_op jit(solution)/shard_map/all_to_all | solution.py:286
  81.0 0.0 collective-permute-done.1.later_ref
  81.0 0.0 collective-permute-done.prior_ref
  81.0 0.0 copy-done
  81.0 9.4 %attend.1 = bf16[32,64,128]{2,1,0:T(8,128)(2,1)S(1)} custom-call(s32[16,256]{1,0:T(8,128)S(1)} %copy-done, f32[1]{0:T(128)} %dynamic_slice.3.slope_ref, bf16[32,64,128]{2,1,0:T(8,128)(2,1)S(1)} %all-to-all-done.1.q_ref, bf16[32,128,128]{2,1,0:T(8,128)(2,1)} %collective-permute-done.prior_ref, bf16[32,128,128]{2,1,0:T(8,128)(2,1)S(1)} %all-to-all-done.own_ref, ...), custom_call_target="tpu_custom_call" | custom-call | tf_op jit(solution)/shard_map/attend/pallas_call | solution.py:269
  90.4 21.9 %all_to_all.15.in_ref = bf16[32,64,128]{2,1,0:T(8,128)(2,1)S(1)} all-to-all(bf16[32,64,128]{2,1,0:T(8,128)(2,1)S(1)} %attend.1), channel_id=1, replica_groups=mesh['blk'=8,'head'=32] {'head'}, dimensions={0} | all-to-all | bytes 1048576 | tf_op jit(solution)/shard_map/all_to_all | solution.py:286
  112.4 1.0 unpack.1
Async XLA Ops:
  2.3 40.9 %all-to-all-start = ((bf16[32,128,128]{2,1,0:T(8,128)(2,1)}), bf16[32,128,128]{2,1,0:T(8,128)(2,1)S(1)}, u32[]{:S(2)}, u32[]{:S(2)}) async-start(bf16[32,128,128]{2,1,0:T(8,128)(2,1)} %pack_kv.1), calls=%async_computation | async-start | bytes 2097152 | tf_op jit(solution)/shard_map/all_to_all | solution.py:286
  43.2 37.8 %collective-permute-start.1 = (bf16[32,128,128]{2,1,0:T(8,128)(2,1)S(1)}, bf16[32,128,128]{2,1,0:T(8,128)(2,1)S(1)}, u32[]{:S(2)}, u32[]{:S(2)}) collective-permute-start(bf16[32,128,128]{2,1,0:T(8,128)(2,1)S(1)} %all-to-all-done.own_ref), channel_id=1, source_target_pairs={{0,224},{32,0},{64,32},{96,64},{128,96},{160,128},{192,160},{224,1... | collective-permute-start | bytes 3145736 | tf_op jit(solution)/shard_map/ppermute | solution.py:31
  45.8 35.2 %collective-permute-start = (bf16[32,128,128]{2,1,0:T(8,128)(2,1)S(1)}, bf16[32,128,128]{2,1,0:T(8,128)(2,1)}, u32[]{:S(2)}, u32[]{:S(2)}) collective-permute-start(bf16[32,128,128]{2,1,0:T(8,128)(2,1)S(1)} %all-to-all-done.own_ref), channel_id=1, source_target_pairs={{0,32},{32,64},{64,96},{96,128},{128,160},{160,192},{192,224},{224... | collective-permute-start | bytes 3145736 | tf_op jit(solution)/shard_map/ppermute | solution.py:31
  45.8 35.2 %copy-start = (s32[16,256]{1,0:T(8,128)S(1)}, s32[16,256]{1,0:T(8,128)}, u32[]{:S(2)}) copy-start(s32[16,256]{1,0:T(8,128)} %table.1.table_ref) | copy-start | bytes 49156
  45.8 35.2 %all-to-all-start.1 = ((bf16[32,64,128]{2,1,0:T(8,128)(2,1)}), bf16[32,64,128]{2,1,0:T(8,128)(2,1)S(1)}, u32[]{:S(2)}, u32[]{:S(2)}) async-start(bf16[32,64,128]{2,1,0:T(8,128)(2,1)} %pack_q.1), calls=%async_computation.1 | async-start | bytes 1048576 | tf_op jit(solution)/shard_map/all_to_all | solution.py:286
  52.6 0.7 copy-start.1

commit v2 on v1

--- a/solution.py
+++ b/solution.py
@@ -25,13 +25,25 @@
 i32 = jnp.int32
 
 
-def from_behind(value, axis, steps):
-    count = lax.axis_size(axis)
-    pairs = [(source, (source + steps) % count) for source in range(count)]
-    return lax.ppermute(value, axis, pairs)
-
-
-def pack_kv_kernel(k_hbm, v_hbm, kv_hbm, k_ref, v_ref, kv_ref, k_sem, v_sem, kv_sem):
+def place_of(head, swap):
+    if head % 2 == 0:
+        return head
+    return head - swap if head & 2 else head + swap
+
+
+def from_behind(value, steps):
+    blocks, heads = lax.axis_size("blk"), lax.axis_size("head")
+    pairs = []
+    for block in range(blocks):
+        target = (block + steps) % blocks
+        crosses = 2 * block // blocks != 2 * target // blocks
+        for place in range(heads):
+            other = place ^ 2 if crosses and place % 2 else place
+            pairs.append((block * heads + place, target * heads + other))
+    return lax.ppermute(value, ("blk", "head"), pairs)
+
+
+def pack_kv_kernel(swap_ref, k_hbm, v_hbm, kv_hbm, k_ref, v_ref, kv_ref, k_sem, v_sem, kv_sem):
     width = HEADS * HD // PARTS
     heads = HEADS // PARTS
     loads, stores = [], []
@@ -47,7 +59,8 @@
         loads[part][1].wait()
         for pair in range(heads // 2):
             columns = slice(pair * 128, pair * 128 + 128)
-            one, two = part * heads + 2 * pair, part * heads + 2 * pair + 1
+            one = part * heads + 2 * pair
+            two = place_of(one + 1, swap_ref[0])
             k = k_ref[part, :, columns]
             upper, lower = k[:64], k[64:]
             kv_ref[one, :64, :] = jnp.concatenate([upper[:, :64], lower[:, :64]], axis=1)
@@ -63,48 +76,53 @@
         store.wait()
 
 
-def pack_kv(keys, values):
+def pack_kv(swap, keys, values):
     anywhere = pl.BlockSpec(memory_space=pl.ANY)
     return pl.pallas_call(
         pack_kv_kernel,
         out_shape=jax.ShapeDtypeStruct((HEADS, 128, 128), bf16),
-        in_specs=[anywhere] * 2,
+        in_specs=[pl.BlockSpec(memory_space=pltpu.SMEM)] + [anywhere] * 2,
         out_specs=anywhere,
         scratch_shapes=[pltpu.VMEM((PARTS, 128, HEADS * HD // PARTS), bf16)] * 2
         + [pltpu.VMEM((HEADS, 128, 128), bf16)]
         + [pltpu.SemaphoreType.DMA((PARTS,))] * 3,
         name="pack_kv",
-    )(keys, values)
-
-
-def pack_q_kernel(q_ref, out_ref):
+    )(swap, keys, values)
+
+
+def pack_q_kernel(swap_ref, q_ref, out_ref):
     for pair in range(HEADS // 2):
         q = q_ref[:, pair * 128 : pair * 128 + 128].T
         out_ref[2 * pair] = q[:64]
-        out_ref[2 * pair + 1] = q[64:]
-
-
-def pack_q(queries):
+        out_ref[place_of(2 * pair + 1, swap_ref[0])] = q[64:]
+
+
+def pack_q(swap, queries):
     return pl.pallas_call(
         pack_q_kernel,
         out_shape=jax.ShapeDtypeStruct((HEADS, HD, 128), bf16),
+        in_specs=[pl.BlockSpec(memory_space=pltpu.SMEM), pl.BlockSpec(memory_space=pltpu.VMEM)],
+        out_specs=pl.BlockSpec(memory_space=pltpu.VMEM),
         name="pack_q",
-    )(queries)
-
-
-def unpack_kernel(in_ref, out_ref):
+    )(swap, queries)
+
+
+def unpack_kernel(swap_ref, in_ref, out_ref):
     for pair in range(HEADS // 2):
-        both = jnp.concatenate([in_ref[2 * pair], in_ref[2 * pair + 1]], axis=0)
+        two = place_of(2 * pair + 1, swap_ref[0])
+        both = jnp.concatenate([in_ref[2 * pair], in_ref[two]], axis=0)
         out_ref[:, pair * 128 : pair * 128 + 128] = both.T
 
 
-def unpack(array):
+def unpack(swap, array):
     return pl.pallas_call(
         unpack_kernel,
         out_shape=jax.ShapeDtypeStruct((128, HEADS * HD), bf16),
+        in_specs=[pl.BlockSpec(memory_space=pltpu.SMEM), pl.BlockSpec(memory_space=pltpu.VMEM)],
+        out_specs=pl.BlockSpec(memory_space=pltpu.VMEM),
         compiler_params=pltpu.CompilerParams(vmem_limit_bytes=8 * 2**20),
         name="unpack",
-    )(array)
+    )(swap, array)
 
 
 def iota(shape, dim):
@@ -288,16 +306,19 @@
 
 def per_device(queries, keys, values, slopes, layer, mask, perm):
     block = lax.axis_index("blk").astype(i32).reshape(1)
-    slope = lax.dynamic_slice_in_dim(slopes, lax.axis_index("head"), 1)
-    own = exchange(pack_kv(keys, values))
-    packed = pack_q(queries)
+    place = lax.axis_index("head").astype(i32).reshape(1)
+    swap = jnp.where(block < lax.axis_size("blk") // 2, 0, 2)
+    head = jnp.where(place % 2 == 0, place, place ^ swap)
+    slope = lax.dynamic_slice_in_dim(slopes, head[0], 1)
+    own = exchange(pack_kv(swap, keys, values))
+    packed = pack_q(swap, queries)
     steps = table(block, perm, layer, mask)
-    own, packed, steps = lax.optimization_barrier((own, packed, steps))
-    prior = from_behind(own, "blk", 1)
-    later = from_behind(own, "blk", -1)
+    own, packed, steps, slope = lax.optimization_barrier((own, packed, steps, slope))
+    prior = from_behind(own, 1)
+    later = from_behind(own, -1)
     q = exchange(packed)
     mixed = attend(steps, slope, q, prior, own, later)
-    return unpack(exchange(mixed))
+    return unpack(swap, exchange(mixed))
 
 
 def solution(mesh):

time: 114 us -> 107 us (0.939)
  waiting for transfers between devices: 50.8 us -> 28.8 us
  blocking collectives: 21.9 us -> 42.7 us
  starting transfers between devices: 22.2 us -> 17.8 us
    all_to_all x2 -> x1, waiting for transfers between devices: 50.8 us -> 22.3 us  [exchange(): lax.all_to_all(array, 'head', split_axis=0, concat_axis=0, tiled=True)]
    all_to_all x1 -> x2, blocking collectives: 21.9 us -> 42.7 us  [exchange(): lax.all_to_all(array, 'head', split_axis=0, concat_axis=0, tiled=True)]
    all_to_all x2 -> x1, starting transfers between devices: 19.6 us -> 12.8 us  [exchange(): lax.all_to_all(array, 'head', split_axis=0, concat_axis=0, tiled=True)]
    ppermute x2, waiting for transfers between devices: 0.01 us -> 6.41 us  [from_behind(): return lax.ppermute(value, ('blk', 'head'), pairs)]
    ppermute x2, starting transfers between devices: 2.59 us -> 5.02 us  [from_behind(): return lax.ppermute(value, ('blk', 'head'), pairs)]
  transfers between devices with their start and end apart: 4 -> 3, of which waited for: 2 -> 3; matrix products, arithmetic and copies ran while one was open for 1% -> 1% of each run, Pallas kernels for 4% -> 4%
where the time goes in v2:
time: 107 us
  blocking collectives  42.7 us (40%)
  waiting for transfers between devices  28.8 us (27%)
  starting transfers between devices  17.8 us (17%)
  Pallas kernels  16.2 us (15%)
  local copies, waits for them, and re-layouts  1.3 us (1%)
    all_to_all x2, blocking collectives, exchange(): lax.all_to_all(array, 'head', split_axis=0, concat_axis=0, tiled=True)  42.7 us
    all_to_all x1, waiting for transfers between devices, exchange(): lax.all_to_all(array, 'head', split_axis=0, concat_axis=0, tiled=True)  22.3 us
    all_to_all x1, starting transfers between devices, exchange(): lax.all_to_all(array, 'head', split_axis=0, concat_axis=0, tiled=True)  12.8 us
    pallas_call x1, Pallas kernels, attend(): pl.pallas_call(attend_kernel, out_shape=jax.ShapeDtypeStruct((TB, HD, TIL...  8.38 us
    ppermute x2, waiting for transfers between devices, from_behind(): return lax.ppermute(value, ('blk', 'head'), pairs)  6.41 us
    ppermute x2, starting transfers between devices, from_behind(): return lax.ppermute(value, ('blk', 'head'), pairs)  5.02 us
    pallas_call x1, Pallas kernels, table(): pl.pallas_call(table_kernel, out_shape=jax.ShapeDtypeStruct((16, MOST_STE...  2.45 us
    pallas_call x1, Pallas kernels, pack_kv(): pl.pallas_call(pack_kv_kernel, out_shape=jax.ShapeDtypeStruct((HEADS, 128...  2.31 us
  transfers between devices with their start and end apart: 3, of which 3 were waited for; matrix products, arithmetic and copies ran while one was open for 1% of the time, Pallas kernels for 4%

profile of v2, /device:TPU:1, one launch (start us, length us, event | category | flops | bytes accessed | tf_op | source)
XLA Modules:
  0.0 106.7 jit_solution(5751572333262664244)
XLA Ops:
  0.0 2.3 %pack_kv.1 = bf16[32,128,128]{2,1,0:T(8,128)(2,1)} custom-call(s32[1]{0:T(128)S(6)} %select_n.18.swap_ref, bf16[128,2048]{1,0:T(8,128)(2,1)} %k_hbm.1, bf16[128,2048]{1,0:T(8,128)(2,1)} %v_hbm.1), custom_call_target="tpu_custom_call" | custom-call | tf_op jit(solution)/shard_map/pack_kv/pallas_call | solution.py:81
  2.3 12.8 %all-to-all-start = ((bf16[32,128,128]{2,1,0:T(8,128)(2,1)}), bf16[32,128,128]{2,1,0:T(8,128)(2,1)S(1)}, u32[]{:S(2)}, u32[]{:S(2)}) async-start(bf16[32,128,128]{2,1,0:T(8,128)(2,1)} %pack_kv.1), calls=%async_computation | async-start | bytes 2097152 | tf_op jit(solution)/shard_map/all_to_all | solution.py:304
  15.1 2.0 %pack_q.1 = bf16[32,64,128]{2,1,0:T(8,128)(2,1)} custom-call(s32[1]{0:T(128)S(6)} %select_n.18.swap_ref, bf16[128,2048]{1,0:T(8,128)(2,1)} %q_ref.1), custom_call_target="tpu_custom_call" | custom-call | tf_op jit(solution)/shard_map/pack_q/pallas_call | solution.py:101
  17.1 0.0 copy-start.1
  17.2 0.7 copy-done.1
  17.8 0.6 dynamic_slice.3.slope_ref
  18.4 2.4 %table.1.table_ref = s32[16,256]{1,0:T(8,128)} custom-call(s32[1]{0:T(128)} %bitcast.block_ref, s32[1,256]{1,0:T(1,128)} %bitcast.5, s32[1,256]{1,0:T(1,128)} %bitcast.6, s32[256,256]{1,0:T(8,128)} %mask_ref.1), custom_call_target="tpu_custom_call" | custom-call | tf_op jit(solution)/shard_map/table/pallas_call | solution.py:186
  20.9 0.0 copy-start
  20.9 22.3 %all-to-all-done.own_ref = bf16[32,128,128]{2,1,0:T(8,128)(2,1)S(1)} async-done(((bf16[32,128,128]{2,1,0:T(8,128)(2,1)}), bf16[32,128,128]{2,1,0:T(8,128)(2,1)S(1)}, u32[]{:S(2)}, u32[]{:S(2)}) %all-to-all-start) | async-done | bytes 1048608 | tf_op jit(solution)/shard_map/all_to_all | solution.py:304
  43.2 5.0 %collective-permute-start.1 = (bf16[32,128,128]{2,1,0:T(8,128)(2,1)S(1)}, bf16[32,128,128]{2,1,0:T(8,128)(2,1)S(1)}, u32[]{:S(2)}, u32[]{:S(2)}) collective-permute-start(bf16[32,128,128]{2,1,0:T(8,128)(2,1)S(1)} %all-to-all-done.own_ref), channel_id=1, source_target_pairs={{0,224},{1,227},{2,226},{3,225},{4,228},{5,231},{6,230},{7,229},{8... | collective-permute-start | bytes 3145736 | tf_op jit(solution)/shard_map/ppermute | solution.py:43
  48.3 0.0 collective-permute-start
  48.3 21.3 %all_to_all.15.q_ref = bf16[32,64,128]{2,1,0:T(8,128)(2,1)S(1)} all-to-all(bf16[32,64,128]{2,1,0:T(8,128)(2,1)} %pack_q.1), channel_id=1, replica_groups=mesh['blk'=8,'head'=32] {'head'}, dimensions={0} | all-to-all | bytes 1048576 | tf_op jit(solution)/shard_map/all_to_all | solution.py:304
  69.5 0.9 collective-permute-done.1.later_ref
  70.5 5.5 %collective-permute-done.prior_ref = bf16[32,128,128]{2,1,0:T(8,128)(2,1)S(1)} collective-permute-done((bf16[32,128,128]{2,1,0:T(8,128)(2,1)S(1)}, bf16[32,128,128]{2,1,0:T(8,128)(2,1)S(1)}, u32[]{:S(2)}, u32[]{:S(2)}) %collective-permute-start) | collective-permute-done | bytes 1048608 | tf_op jit(solution)/shard_map/ppermute | solution.py:43
  75.9 0.0 copy-done
  75.9 8.4 %attend.1 = bf16[32,64,128]{2,1,0:T(8,128)(2,1)S(1)} custom-call(s32[16,256]{1,0:T(8,128)S(1)} %copy-done, f32[1]{0:T(128)} %dynamic_slice.3.slope_ref, bf16[32,64,128]{2,1,0:T(8,128)(2,1)S(1)} %all_to_all.15.q_ref, bf16[32,128,128]{2,1,0:T(8,128)(2,1)S(1)} %collective-permute-done.prior_ref, bf16[32,128,128]{2,1,0:T(8,128)(2,1)S(1)} %all-to-all-done.own_ref, ...), custom_call_target="tpu_custom_call" | custom-call | tf_op jit(solution)/shard_map/attend/pallas_call | solution.py:287
  84.3 21.4 %all_to_all.16.in_ref = bf16[32,64,128]{2,1,0:T(8,128)(2,1)S(1)} all-to-all(bf16[32,64,128]{2,1,0:T(8,128)(2,1)S(1)} %attend.1), channel_id=1, replica_groups=mesh['blk'=8,'head'=32] {'head'}, dimensions={0} | all-to-all | bytes 1048576 | tf_op jit(solution)/shard_map/all_to_all | solution.py:304
  105.8 1.0 unpack.1
Async XLA Ops:
  2.3 40.9 %all-to-all-start = ((bf16[32,128,128]{2,1,0:T(8,128)(2,1)}), bf16[32,128,128]{2,1,0:T(8,128)(2,1)S(1)}, u32[]{:S(2)}, u32[]{:S(2)}) async-start(bf16[32,128,128]{2,1,0:T(8,128)(2,1)} %pack_kv.1), calls=%async_computation | async-start | bytes 2097152 | tf_op jit(solution)/shard_map/all_to_all | solution.py:304
  17.1 0.7 copy-start.1
  20.9 55.0 %copy-start = (s32[16,256]{1,0:T(8,128)S(1)}, s32[16,256]{1,0:T(8,128)}, u32[]{:S(2)}) copy-start(s32[16,256]{1,0:T(8,128)} %table.1.table_ref) | copy-start | bytes 49156
  43.2 27.2 %collective-permute-start.1 = (bf16[32,128,128]{2,1,0:T(8,128)(2,1)S(1)}, bf16[32,128,128]{2,1,0:T(8,128)(2,1)S(1)}, u32[]{:S(2)}, u32[]{:S(2)}) collective-permute-start(bf16[32,128,128]{2,1,0:T(8,128)(2,1)S(1)} %all-to-all-done.own_ref), channel_id=1, source_target_pairs={{0,224},{1,227},{2,226},{3,225},{4,228},{5,231},{6,230},{7,229},{8... | collective-permute-start | bytes 3145736 | tf_op jit(solution)/shard_map/ppermute | solution.py:43
  48.3 27.7 %collective-permute-start = (bf16[32,128,128]{2,1,0:T(8,128)(2,1)S(1)}, bf16[32,128,128]{2,1,0:T(8,128)(2,1)S(1)}, u32[]{:S(2)}, u32[]{:S(2)}) collective-permute-start(bf16[32,128,128]{2,1,0:T(8,128)(2,1)S(1)} %all-to-all-done.own_ref), channel_id=1, source_target_pairs={{0,32},{1,33},{2,34},{3,35},{4,36},{5,37},{6,38},{7,39},{8,40},{9,... | collective-permute-start | bytes 3145736 | tf_op jit(solution)/shard_map/ppermute | solution.py:43

commit v3 on v2

--- a/solution.py
+++ b/solution.py
@@ -31,11 +31,11 @@
     return head - swap if head & 2 else head + swap
 
 
-def from_behind(value, steps):
+def swapped(value, odd):
     blocks, heads = lax.axis_size("blk"), lax.axis_size("head")
     pairs = []
     for block in range(blocks):
-        target = (block + steps) % blocks
+        target = (block + (1 if block % 2 == odd else -1)) % blocks
         crosses = 2 * block // blocks != 2 * target // blocks
         for place in range(heads):
             other = place ^ 2 if crosses and place % 2 else place
@@ -195,19 +195,23 @@
 def attend_kernel(
     table_ref,
     slope_ref,
+    block_ref,
     q_ref,
-    prior_ref,
+    first_ref,
     own_ref,
-    later_ref,
+    second_ref,
     out_ref,
     kv,
     arrived,
     *buffers,
 ):
     scores, weights = buffers[: 2 * UNROLL], buffers[2 * UNROLL :]
+    side = pl.multiple_of(lax.rem(block_ref[0], 2) * (2 * TB), TB)
     copies = [
-        pltpu.make_async_copy(source, kv.at[pl.ds(index * TB, TB)], arrived.at[index])
-        for index, source in enumerate((prior_ref, own_ref, later_ref))
+        pltpu.make_async_copy(source, kv.at[pl.ds(place, TB)], arrived.at[index])
+        for index, (source, place) in enumerate(
+            ((first_ref, side), (own_ref, TB), (second_ref, 2 * TB - side))
+        )
     ]
     for copy in copies:
         copy.start()
@@ -280,14 +284,14 @@
     lax.fori_loop(0, pairs, body, (row, jnp.zeros((HD + 16, TILE), f32), (row,) * (2 * UNROLL)))
 
 
-def attend(steps, slope, q, prior, own, later):
+def attend(steps, slope, block, q, first, own, second):
     smem = pl.BlockSpec(memory_space=pltpu.SMEM)
     vmem = pl.BlockSpec(memory_space=pltpu.VMEM)
     anywhere = pl.BlockSpec(memory_space=pl.ANY)
     return pl.pallas_call(
         attend_kernel,
         out_shape=jax.ShapeDtypeStruct((TB, HD, TILE), bf16),
-        in_specs=[smem, smem, vmem, anywhere, anywhere, anywhere],
+        in_specs=[smem, smem, smem, vmem, anywhere, anywhere, anywhere],
         out_specs=vmem,
         scratch_shapes=[
             pltpu.VMEM((3 * TB, 2 * HD, TILE), bf16),
@@ -297,7 +301,7 @@
         + [pltpu.VMEM((GROUP * TILE, TILE), bf16)] * (2 * UNROLL),
         compiler_params=pltpu.CompilerParams(vmem_limit_bytes=12 * 2**20),
         name="attend",
-    )(steps, slope, q, prior, own, later)
+    )(steps, slope, block, q, first, own, second)
 
 
 def exchange(array):
@@ -314,10 +318,10 @@
     packed = pack_q(swap, queries)
     steps = table(block, perm, layer, mask)
     own, packed, steps, slope = lax.optimization_barrier((own, packed, steps, slope))
-    prior = from_behind(own, 1)
-    later = from_behind(own, -1)
+    first = swapped(own, 1)
+    second = swapped(own, 0)
     q = exchange(packed)
-    mixed = attend(steps, slope, q, prior, own, later)
+    mixed = attend(steps, slope, block, q, first, own, second)
     return unpack(swap, exchange(mixed))
 
 

time: 107 us -> 106 us (level); the launches traced: 107 us -> 104 us
  waiting for transfers between devices: 28.8 us -> 23.3 us
  blocking collectives: 42.7 us -> 44.9 us
    ppermute x2, waiting for transfers between devices: 6.41 us -> 0.96 us  [swapped(): return lax.ppermute(value, ('blk', 'head'), pairs)]
    all_to_all x2, blocking collectives: 42.7 us -> 44.9 us  [exchange(): lax.all_to_all(array, 'head', split_axis=0, concat_axis=0, tiled=True)]
  transfers between devices with their start and end apart: 3 -> 3, of which waited for: 3 -> 2; matrix products, arithmetic and copies ran while one was open for 1% -> 1% of each run, Pallas kernels for 4% -> 4%
where the time goes in v3:
time: 106 us; the launch traced here: 104 us
  blocking collectives  44.9 us (42%)
  waiting for transfers between devices  23.3 us (22%)
  starting transfers between devices  18.3 us (17%)
  Pallas kernels  16.1 us (15%)
  local copies, waits for them, and re-layouts  1.3 us (1%)
    all_to_all x2, blocking collectives, exchange(): lax.all_to_all(array, 'head', split_axis=0, concat_axis=0, tiled=True)  44.9 us
    all_to_all x1, waiting for transfers between devices, exchange(): lax.all_to_all(array, 'head', split_axis=0, concat_axis=0, tiled=True)  22.3 us
    all_to_all x1, starting transfers between devices, exchange(): lax.all_to_all(array, 'head', split_axis=0, concat_axis=0, tiled=True)  12.8 us
    pallas_call x1, Pallas kernels, attend(): pl.pallas_call(attend_kernel, out_shape=jax.ShapeDtypeStruct((TB, HD, TIL...  8.38 us
    ppermute x2, starting transfers between devices, swapped(): return lax.ppermute(value, ('blk', 'head'), pairs)  5.56 us
    pallas_call x1, Pallas kernels, table(): pl.pallas_call(table_kernel, out_shape=jax.ShapeDtypeStruct((16, MOST_STE...  2.45 us
    pallas_call x1, Pallas kernels, pack_kv(): pl.pallas_call(pack_kv_kernel, out_shape=jax.ShapeDtypeStruct((HEADS, 128...  2.31 us
  transfers between devices with their start and end apart: 3, of which 2 were waited for; matrix products, arithmetic and copies ran while one was open for 1% of the time, Pallas kernels for 4%

profile of v3, /device:TPU:1, one launch (start us, length us, event | category | flops | bytes accessed | tf_op | source)
XLA Modules:
  0.0 104.0 jit_solution(9386578002457014072)
XLA Ops:
  0.0 2.3 %pack_kv.1 = bf16[32,128,128]{2,1,0:T(8,128)(2,1)} custom-call(s32[1]{0:T(128)S(6)} %select_n.18.swap_ref, bf16[128,2048]{1,0:T(8,128)(2,1)} %k_hbm.1, bf16[128,2048]{1,0:T(8,128)(2,1)} %v_hbm.1), custom_call_target="tpu_custom_call" | custom-call | tf_op jit(solution)/shard_map/pack_kv/pallas_call | solution.py:81
  2.3 12.8 %all-to-all-start = ((bf16[32,128,128]{2,1,0:T(8,128)(2,1)}), bf16[32,128,128]{2,1,0:T(8,128)(2,1)S(1)}, u32[]{:S(2)}, u32[]{:S(2)}) async-start(bf16[32,128,128]{2,1,0:T(8,128)(2,1)} %pack_kv.1), calls=%async_computation | async-start | bytes 2097152 | tf_op jit(solution)/shard_map/all_to_all | solution.py:308
  15.1 2.0 %pack_q.1 = bf16[32,64,128]{2,1,0:T(8,128)(2,1)} custom-call(s32[1]{0:T(128)S(6)} %select_n.18.swap_ref, bf16[128,2048]{1,0:T(8,128)(2,1)} %q_ref.1), custom_call_target="tpu_custom_call" | custom-call | tf_op jit(solution)/shard_map/pack_q/pallas_call | solution.py:101
  17.1 0.0 copy-start.1
  17.2 0.7 copy-done.1
  17.8 0.6 dynamic_slice.3.slope_ref
  18.4 2.4 %table.1.table_ref = s32[16,256]{1,0:T(8,128)} custom-call(s32[1]{0:T(128)} %bitcast.block_ref, s32[1,256]{1,0:T(1,128)} %bitcast.5, s32[1,256]{1,0:T(1,128)} %bitcast.6, s32[256,256]{1,0:T(8,128)} %mask_ref.1), custom_call_target="tpu_custom_call" | custom-call | tf_op jit(solution)/shard_map/table/pallas_call | solution.py:186
  20.9 0.0 copy-start
  20.9 22.3 %all-to-all-done.own_ref = bf16[32,128,128]{2,1,0:T(8,128)(2,1)S(1)} async-done(((bf16[32,128,128]{2,1,0:T(8,128)(2,1)}), bf16[32,128,128]{2,1,0:T(8,128)(2,1)S(1)}, u32[]{:S(2)}, u32[]{:S(2)}) %all-to-all-start) | async-done | bytes 1048608 | tf_op jit(solution)/shard_map/all_to_all | solution.py:308
  43.2 1.2 %collective-permute-start.1 = (bf16[32,128,128]{2,1,0:T(8,128)(2,1)S(1)}, bf16[32,128,128]{2,1,0:T(8,128)(2,1)S(1)}, u32[]{:S(2)}, u32[]{:S(2)}) collective-permute-start(bf16[32,128,128]{2,1,0:T(8,128)(2,1)S(1)} %all-to-all-done.own_ref), channel_id=1, source_target_pairs={{0,32},{1,33},{2,34},{3,35},{4,36},{5,37},{6,38},{7,39},{8,40},{9,... | collective-permute-start | bytes 3145736 | tf_op jit(solution)/shard_map/ppermute | solution.py:43
  44.5 4.4 %collective-permute-start = (bf16[32,128,128]{2,1,0:T(8,128)(2,1)S(1)}, bf16[32,128,128]{2,1,0:T(8,128)(2,1)S(1)}, u32[]{:S(2)}, u32[]{:S(2)}) collective-permute-start(bf16[32,128,128]{2,1,0:T(8,128)(2,1)S(1)} %all-to-all-done.own_ref), channel_id=1, source_target_pairs={{0,224},{1,227},{2,226},{3,225},{4,228},{5,231},{6,230},{7,229},{8... | collective-permute-start | bytes 3145736 | tf_op jit(solution)/shard_map/ppermute | solution.py:43
  48.8 21.5 %all_to_all.15.q_ref = bf16[32,64,128]{2,1,0:T(8,128)(2,1)S(1)} all-to-all(bf16[32,64,128]{2,1,0:T(8,128)(2,1)} %pack_q.1), channel_id=1, replica_groups=mesh['blk'=8,'head'=32] {'head'}, dimensions={0} | all-to-all | bytes 1048576 | tf_op jit(solution)/shard_map/all_to_all | solution.py:308
  70.3 0.0 collective-permute-done.1.second_ref
  70.3 1.0 collective-permute-done.first_ref
  71.3 0.0 copy-done
  71.3 8.4 %attend.1 = bf16[32,64,128]{2,1,0:T(8,128)(2,1)S(1)} custom-call(s32[16,256]{1,0:T(8,128)S(1)} %copy-done, f32[1]{0:T(128)} %dynamic_slice.3.slope_ref, s32[1]{0:T(128)} %bitcast.block_ref, bf16[32,64,128]{2,1,0:T(8,128)(2,1)S(1)} %all_to_all.15.q_ref, bf16[32,128,128]{2,1,0:T(8,128)(2,1)S(1)} %collective-permute-done.first_ref, ...), custom_call_target="tpu_custom_call" | custom-call | tf_op jit(solution)/shard_map/attend/pallas_call | solution.py:291
  79.7 23.4 %all_to_all.16.in_ref = bf16[32,64,128]{2,1,0:T(8,128)(2,1)S(1)} all-to-all(bf16[32,64,128]{2,1,0:T(8,128)(2,1)S(1)} %attend.1), channel_id=1, replica_groups=mesh['blk'=8,'head'=32] {'head'}, dimensions={0} | all-to-all | bytes 1048576 | tf_op jit(solution)/shard_map/all_to_all | solution.py:308
  103.0 1.0 unpack.1
Async XLA Ops:
  2.3 40.9 %all-to-all-start = ((bf16[32,128,128]{2,1,0:T(8,128)(2,1)}), bf16[32,128,128]{2,1,0:T(8,128)(2,1)S(1)}, u32[]{:S(2)}, u32[]{:S(2)}) async-start(bf16[32,128,128]{2,1,0:T(8,128)(2,1)} %pack_kv.1), calls=%async_computation | async-start | bytes 2097152 | tf_op jit(solution)/shard_map/all_to_all | solution.py:308
  17.1 0.7 copy-start.1
  20.9 50.4 %copy-start = (s32[16,256]{1,0:T(8,128)S(1)}, s32[16,256]{1,0:T(8,128)}, u32[]{:S(2)}) copy-start(s32[16,256]{1,0:T(8,128)} %table.1.table_ref) | copy-start | bytes 49156
  43.2 27.1 %collective-permute-start.1 = (bf16[32,128,128]{2,1,0:T(8,128)(2,1)S(1)}, bf16[32,128,128]{2,1,0:T(8,128)(2,1)S(1)}, u32[]{:S(2)}, u32[]{:S(2)}) collective-permute-start(bf16[32,128,128]{2,1,0:T(8,128)(2,1)S(1)} %all-to-all-done.own_ref), channel_id=1, source_target_pairs={{0,32},{1,33},{2,34},{3,35},{4,36},{5,37},{6,38},{7,39},{8,40},{9,... | collective-permute-start | bytes 3145736 | tf_op jit(solution)/shard_map/ppermute | solution.py:43
  44.5 26.9 %collective-permute-start = (bf16[32,128,128]{2,1,0:T(8,128)(2,1)S(1)}, bf16[32,128,128]{2,1,0:T(8,128)(2,1)S(1)}, u32[]{:S(2)}, u32[]{:S(2)}) collective-permute-start(bf16[32,128,128]{2,1,0:T(8,128)(2,1)S(1)} %all-to-all-done.own_ref), channel_id=1, source_target_pairs={{0,224},{1,227},{2,226},{3,225},{4,228},{5,231},{6,230},{7,229},{8... | collective-permute-start | bytes 3145736 | tf_op jit(solution)/shard_map/ppermute | solution.py:43
